TPU v7x, 32 devices: a whole 2x2x4 slice. The times are simulated.
32 devices in a mesh: row: 8 (over z, x), col: 4 (over y, core).
Axes of the slice: x: 2, y: 2, z: 4, core: 2. Of those that a mesh axis runs over, the one named last changes fastest.
Arguments:
- diagonal_inverses: bfloat16 [24, 2048, 2048], P('row', 'col'), may hold values from -0.125 to 0.125
- column_basis: bfloat16 [24, 2048, 256], P('row', 'col'), may hold values from -6 to 6
- row_basis: bfloat16 [24, 2048, 256], P('row', 'col'), may hold values from -0.125 to 0.125
- transfer: float32 [24, 256, 256], P('row', 'col'), may hold values from -0.375 to 0.375
- coupling: float32 [24, 256, 256], P('row', 'col'), may hold values from -6 to 6
- ranks: int32 [24], P('row'), may hold values from 128 to 256, as said below
Outputs:
- merged: float32 [24, 256, 256], P('row', 'col')
- parent_skeleton: float32 [24, 256, 256], P('row', 'col')
Inputs may be any that keep to these rules, and one draw needn't show every extreme that they name: `ranks`: each rank is 128 or 256; both occur in every draw.
All inputs are finite; a program needn't handle non-finite values.
Results may differ from a plain program's by a relative error of at most 0.0021.
Values may be sent and summed in bfloat16 or wider, within the bound.
A program may use at most 64 MiB of HBM per device.

v0:
```python
import jax
import jax.numpy as jnp
from jax import lax
from jax.sharding import PartitionSpec as P

BIT = 2


def swapped(block, axis, bit):
    count = lax.axis_size(axis)
    route = []
    for low in range(count):
        high = low | 1 << bit
        if high != low and high < count:
            route += [(low, high), (high, low)]
    return lax.ppermute(block, axis, route)


def shards(diagonal_inverses, column_basis, row_basis, transfer, coupling, ranks):
    rank_width = transfer.shape[2]
    part_rows = transfer.shape[1]
    highest = lax.Precision.HIGHEST
    live_cols = jnp.arange(rank_width, dtype=jnp.int32)[None, :] < ranks[:, None]
    left_factor_basis = jnp.where(live_cols[:, None, :], column_basis, jnp.zeros_like(column_basis))
    right_factor_basis = jnp.where(live_cols[:, None, :], row_basis, jnp.zeros_like(row_basis))
    eliminated_part = jnp.einsum(
        "nmp,npr->nmr",
        diagonal_inverses,
        lax.all_gather(left_factor_basis, "col", axis=1, tiled=True),
        preferred_element_type=jnp.float32,
    ).astype(jnp.bfloat16)
    skeleton = jnp.transpose(
        lax.psum_scatter(
            jnp.einsum(
                "hgp,hgd->phd",
                right_factor_basis,
                eliminated_part,
                preferred_element_type=jnp.float32,
            ),
            "col",
            scatter_dimension=0,
            tiled=True,
        ),
        (1, 0, 2),
    )
    offset_rows = lax.axis_index("col") * part_rows
    active_rows = lax.dynamic_slice_in_dim(live_cols, offset_rows, part_rows, 1)
    masked = transfer * active_rows[:, :, None].astype(jnp.float32)
    masked_sib = swapped(masked, "row", BIT)
    complete_local_block, whole_sib = (
        lax.all_gather(masked, "col", axis=1, tiled=True),
        lax.all_gather(masked_sib, "col", axis=1, tiled=True),
    )
    merged = jnp.einsum("nij,njk->nik", skeleton, complete_local_block, precision=highest)
    merged = merged + jnp.einsum("nij,njk->nik", coupling, whole_sib, precision=highest)
    own_term = jnp.transpose(
        lax.psum_scatter(
            jnp.einsum("nji,njk->ink", masked, merged, precision=highest),
            "col",
            scatter_dimension=0,
            tiled=True,
        ),
        (1, 0, 2),
    )
    parent = own_term + swapped(own_term, "row", BIT)
    return (merged, parent)


def solution(mesh):
    placed = (
        P("row", "col", None),
        P("row", "col", None),
        P("row", "col", None),
        P("row", "col", None),
        P("row", "col", None),
        P("row"),
    )
    return jax.shard_map(
        shards,
        mesh=mesh,
        in_specs=placed,
        out_specs=(P("row", "col", None), P("row", "col", None)),
        check_vma=False,
    )
```

profile of v0, /device:TPU:0, one launch (start us, length us, event | category | flops | bytes accessed | tf_op | source)
XLA Modules:
  0.0 138.4 jit_solution(1713739336658735654)
XLA Ops:
  7.2 0.0 copy-start
  7.2 0.0 all-gather.2.cloned.1.call-start
  7.2 0.8 iota_compare_fusion
  8.0 2.1 %broadcast_select_fusion = bf16[3,512,256]{2,1,0:T(8,128)(2,1)} fusion(bf16[3,512,256]{2,1,0:T(8,128)(2,1)} %param.7, pred[3,256]{1,0:T(4,128)(4,1)S(1)} %iota_compare_fusion), kind=kLoop, calls=%fused_computation.7 | loop fusion | flops 393216 | bytes 1573632 | tf_op jit(solution)/shard_map/jit(_where)/select_n | solution.py:24
  10.1 0.0 all-gather.2.cloned.1.call-update
  10.1 0.0 copy-start.2
  10.1 0.0 reduce-scatter.2.cloned.1.call-start
  10.2 31.3 %all-gather.2.cloned.1.call-done = bf16[3,2048,256]{2,1,0:T(8,128)(2,1)} async-done(((bf16[3,512,256]{2,1,0:T(8,128)(2,1)}), bf16[3,2048,256]{2,1,0:T(8,128)(2,1)}) %all-gather.2.cloned.1.call-update) | async-done | bytes 3145744 | tf_op jit(solution)/shard_map/all_gather | solution.py:29
  41.5 7.1 %convolution_bitcast_fusion = f32[256,3,256]{2,0,1:T(8,128)} fusion(bf16[3,2048,256]{2,1,0:T(8,128)(2,1)} %all-gather.2.cloned.1.call-done, bf16[3,512,2048]{2,1,0:T(8,128)(2,1)} %param.6, bf16[3,512,256]{2,1,0:T(8,128)(2,1)} %param.8, pred[3,256]{1,0:T(4,128)(4,1)S(1)} %iota_compare_fusion), kind=kOutput, calls=%fused_computation.1 | convolution fusion | flops 1812725760 | bytes 11010816 | tf_op jit(solution)/shard_map/hgp,hgd->phd/dot_general | solution.py:34
  48.6 0.0 reduce-scatter.2.cloned.1.call-update
  48.6 0.0 all-reduce.3.cloned.1.call-start
  48.7 0.1 dynamic-slice_convert_fusion
  48.8 0.0 copy-done.2
  48.8 0.1 broadcast_multiply_fusion
  48.9 2.5 %collective-permute-start = (f32[3,64,256]{2,1,0:T(8,128)S(1)}, f32[3,64,256]{2,1,0:T(8,128)S(1)}, u32[]{:S(2)}, u32[]{:S(2)}) collective-permute-start(f32[3,64,256]{2,1,0:T(8,128)S(1)} %broadcast_multiply_fusion), channel_id=1, source_target_pairs={{0,16},{16,0},{4,20},{20,4},{8,24},{24,8},{12,28},{28,12},{1,17},{... | collective-permute-start | bytes 589832 | tf_op jit(solution)/shard_map/ppermute | solution.py:16
  51.3 8.3 %all_gather.10 = f32[3,256,256]{2,1,0:T(8,128)S(1)} all-gather(f32[3,64,256]{2,1,0:T(8,128)S(1)} %broadcast_multiply_fusion), channel_id=1, replica_groups=mesh['row'=8,'col'=4] {'col'}, dimensions={1}, use_global_device_ids=true | all-gather | bytes 983040 | tf_op jit(solution)/shard_map/all_gather | solution.py:51
  59.6 1.4 %collective-permute-done = f32[3,64,256]{2,1,0:T(8,128)S(1)} collective-permute-done((f32[3,64,256]{2,1,0:T(8,128)S(1)}, f32[3,64,256]{2,1,0:T(8,128)S(1)}, u32[]{:S(2)}, u32[]{:S(2)}) %collective-permute-start) | collective-permute-done | bytes 196640 | tf_op jit(solution)/shard_map/ppermute | solution.py:16
  61.1 10.0 %all_gather.11 = f32[3,256,256]{2,1,0:T(8,128)S(1)} all-gather(f32[3,64,256]{2,1,0:T(8,128)S(1)} %collective-permute-done), channel_id=1, replica_groups=mesh['row'=8,'col'=4] {'col'}, dimensions={1}, use_global_device_ids=true | all-gather | bytes 983040 | tf_op jit(solution)/shard_map/all_gather | solution.py:52
  71.1 0.0 copy-start.3
  71.1 2.1 %reduce-scatter.2.cloned.1.call-done = f32[64,3,256]{2,0,1:T(8,128)} async-done(((f32[256,3,256]{2,0,1:T(8,128)}), f32[64,3,256]{2,0,1:T(8,128)}) %reduce-scatter.2.cloned.1.call-update) | async-done | bytes 196624 | tf_op jit(solution)/shard_map/reduce_scatter | solution.py:33
  73.2 1.5 %fusion.4 = f32[3,64,256]{2,1,0:T(8,128)S(1)} fusion(f32[3,256,256]{2,1,0:T(8,128)S(1)} %all_gather.10, f32[64,3,256]{2,0,1:T(8,128)} %reduce-scatter.2.cloned.1.call-done), kind=kOutput, calls=%fused_computation.10 | convolution fusion | flops 150994944 | bytes 1179648 | tf_op jit(solution)/shard_map/nij,njk->nik/dot_general | solution.py:54
  74.7 0.0 copy-done
  74.7 0.6 fusion
  75.4 0.0 copy-start.1
  75.4 0.8 convolution_bitcast_fusion.1
  76.2 1.4 copy.9
  77.6 0.0 all-reduce.3.cloned.1.call-update
  77.6 0.0 copy-done.3
  77.6 0.6 dynamic-slice
  78.8 36.0 %all-reduce.3.cloned.1.call-done = f32[256,3,256]{2,1,0:T(4,128)} async-done(((f32[256,3,256]{2,1,0:T(4,128)}), f32[256,3,256]{2,1,0:T(4,128)}) %all-reduce.3.cloned.1.call-update) | async-done | bytes 786448
  114.8 1.0 dynamic-slice_bitcast_fusion
  115.8 2.5 %collective-permute-start.1 = (f32[3,64,256]{2,0,1:T(4,128)S(1)}, f32[3,64,256]{2,0,1:T(4,128)S(1)}, u32[]{:S(2)}, u32[]{:S(2)}) collective-permute-start(f32[3,64,256]{2,0,1:T(4,128)S(1)} %dynamic-slice_bitcast_fusion), channel_id=1, source_target_pairs={{0,16},{16,0},{4,20},{20,4},{8,24},{24,8},{12,28},{28,12},{1,17},{... | collective-permute-start | bytes 589832 | tf_op jit(solution)/shard_map/ppermute | solution.py:16
  118.3 11.8 %collective-permute-done.1 = f32[3,64,256]{2,0,1:T(4,128)S(1)} collective-permute-done((f32[3,64,256]{2,0,1:T(4,128)S(1)}, f32[3,64,256]{2,0,1:T(4,128)S(1)}, u32[]{:S(2)}, u32[]{:S(2)}) %collective-permute-start.1) | collective-permute-done | bytes 196640 | tf_op jit(solution)/shard_map/ppermute | solution.py:16
  130.1 1.0 fusion.14
  131.1 0.7 copy.10
  131.9 0.0 copy-done.1
Async XLA Ops:
  7.2 67.6 %copy-start = (f32[3,64,256]{2,1,0:T(8,128)S(1)}, f32[3,64,256]{2,1,0:T(8,128)}, u32[]{:S(2)}) copy-start(f32[3,64,256]{2,1,0:T(8,128)} %param.10) | copy-start | bytes 589828
  7.2 34.3 %all-gather.2.cloned.1.call-start = ((), (), s32[]{:S(2)}) async-start(), calls=%async_computation.1 | async-start | bytes 3932160 | tf_op jit(solution)/shard_map/all_gather | solution.py:29
  10.1 38.7 %copy-start.2 = (f32[3,64,256]{2,1,0:T(8,128)S(1)}, f32[3,64,256]{2,1,0:T(8,128)}, u32[]{:S(2)}) copy-start(f32[3,64,256]{2,1,0:T(8,128)} %param.9) | copy-start | bytes 589828
  10.1 63.1 %reduce-scatter.2.cloned.1.call-start = ((), (), s32[]{:S(2)}) async-start(), calls=%async_computation.2 | async-start | bytes 983040 | tf_op jit(solution)/shard_map/reduce_scatter | solution.py:33
  48.6 66.2 %all-reduce.3.cloned.1.call-start = ((), (), s32[]{:S(2)}) async-start(), calls=%async_computation.3 | async-start | bytes 2097152
  48.9 12.2 %collective-permute-start = (f32[3,64,256]{2,1,0:T(8,128)S(1)}, f32[3,64,256]{2,1,0:T(8,128)S(1)}, u32[]{:S(2)}, u32[]{:S(2)}) collective-permute-start(f32[3,64,256]{2,1,0:T(8,128)S(1)} %broadcast_multiply_fusion), channel_id=1, source_target_pairs={{0,16},{16,0},{4,20},{20,4},{8,24},{24,8},{12,28},{28,12},{1,17},{... | collective-permute-start | bytes 589832 | tf_op jit(solution)/shard_map/ppermute | solution.py:16
  71.1 6.5 %copy-start.3 = (u32[32]{0:T(128)S(1)}, u32[32]{0:T(128)}, u32[]{:S(2)}) copy-start(u32[32]{0:T(128)} %constant.20) | copy-start | bytes 388
  75.4 56.5 %copy-start.1 = (f32[3,64,256]{2,1,0:T(8,128)}, f32[3,64,256]{2,1,0:T(8,128)S(1)}, u32[]{:S(2)}) copy-start(f32[3,64,256]{2,1,0:T(8,128)S(1)} %fusion) | copy-start | bytes 589828
  115.8 14.3 %collective-permute-start.1 = (f32[3,64,256]{2,0,1:T(4,128)S(1)}, f32[3,64,256]{2,0,1:T(4,128)S(1)}, u32[]{:S(2)}, u32[]{:S(2)}) collective-permute-start(f32[3,64,256]{2,0,1:T(4,128)S(1)} %dynamic-slice_bitcast_fusion), channel_id=1, source_target_pairs={{0,16},{16,0},{4,20},{20,4},{8,24},{24,8},{12,28},{28,12},{1,17},{... | collective-permute-start | bytes 589832 | tf_op jit(solution)/shard_map/ppermute | solution.py:16
Sparse Core Ops, SparseCore 0:
  10.2 31.2 all-gather.1
  48.7 24.3 reduce-scatter.1
  77.7 37.0 all-reduce.2
where the time goes:
time: 139 us; the launch traced here: 138 us
  waiting for transfers between devices  82.7 us (59%)
  blocking collectives  18.3 us (13%)
  between operations  14.5 us (10%)
  matrix products  10.1 us (7%)
  starting transfers between devices  5.07 us (4%)
  other arithmetic  4.03 us (3%)
  local copies, waits for them, and re-layouts  3.68 us (3%)
    unnamed x4, waiting for transfers between devices  36 us
    all_gather x1, waiting for transfers between devices, shards(): lax.all_gather(left_factor_basis, 'col', axis=1, tiled=True)  31.3 us
    ppermute x2, waiting for transfers between devices, swapped(): return lax.ppermute(block, axis, route)  13.3 us
    all_gather x1, blocking collectives, shards(): lax.all_gather(masked_sib, 'col', axis=1, tiled=True)  9.98 us
    all_gather x1, blocking collectives, shards(): lax.all_gather(masked, 'col', axis=1, tiled=True)  8.3 us
    dot_general x1, matrix products, shards(): jnp.einsum('hgp,hgd->phd', right_factor_basis, eliminated_part, preferred...  7.12 us
    ppermute x2, starting transfers between devices, swapped(): return lax.ppermute(block, axis, route)  4.94 us
  transfers between devices with their start and end apart: 5, of which 5 were waited for; matrix products, arithmetic and copies ran while one was open for 1% of the time, Pallas kernels for 0%

commit v1 on v0

--- a/solution.py
+++ b/solution.py
@@ -4,6 +4,19 @@
 from jax.sharding import PartitionSpec as P
 
 BIT = 2
+
+
+def gather_around(x, axis, dim):
+    count, index, span = (lax.axis_size(axis), lax.axis_index(axis), x.shape[dim])
+    ahead = [(i, (i + 1) % count) for i in range(count)]
+    whole = jnp.zeros((*x.shape[:dim], count * span, *x.shape[dim + 1 :]), x.dtype)
+    block = x
+    for step in range(count):
+        owner = (index - step) % count
+        whole = lax.dynamic_update_slice_in_dim(whole, block, owner * span, axis=dim)
+        if step < count - 1:
+            block = lax.ppermute(block, axis, ahead)
+    return whole
 
 
 def swapped(block, axis, bit):
@@ -48,7 +61,7 @@
     masked = transfer * active_rows[:, :, None].astype(jnp.float32)
     masked_sib = swapped(masked, "row", BIT)
     complete_local_block, whole_sib = (
-        lax.all_gather(masked, "col", axis=1, tiled=True),
+        gather_around(masked, "col", 1),
         lax.all_gather(masked_sib, "col", axis=1, tiled=True),
     )
     merged = jnp.einsum("nij,njk->nik", skeleton, complete_local_block, precision=highest)

time: 139 us -> 144 us (1.036)
  waiting for transfers between devices: 82.7 us -> 95.1 us
  blocking collectives: 18.3 us -> 10.5 us
    all_gather x1 -> x0, blocking collectives: 8.3 us -> none  [shards(): lax.all_gather(masked, 'col', axis=1, tiled=True)]
    ppermute x0 -> x3, waiting for transfers between devices: none -> 7.31 us  [gather_around(): block = lax.ppermute(block, axis, ahead)]
    ppermute x2, waiting for transfers between devices: 13.3 us -> 19.1 us  [swapped(): return lax.ppermute(block, axis, route)]
    reduce_scatter x1, waiting for transfers between devices: 2.13 us -> 0.02 us  [shards(): lax.psum_scatter(jnp.einsum('hgp,hgd->phd', right_factor_basis, eliminate...]
  transfers between devices with their start and end apart: 5 -> 8, of which waited for: 5 -> 6; matrix products, arithmetic and copies ran while one was open for 1% -> 1% of each run, Pallas kernels for 0% -> 0%
where the time goes in v1:
time: 144 us
  waiting for transfers between devices  95.1 us (66%)
  between operations  14.5 us (10%)
  blocking collectives  10.5 us (7%)
  matrix products  10.1 us (7%)
  starting transfers between devices  5.69 us (4%)
  other arithmetic  4.06 us (3%)
  local copies, waits for them, and re-layouts  3.77 us (3%)
    unnamed x4, waiting for transfers between devices  37.4 us
    all_gather x1, waiting for transfers between devices, shards(): lax.all_gather(left_factor_basis, 'col', axis=1, tiled=True)  31.3 us
    ppermute x2, waiting for transfers between devices, swapped(): return lax.ppermute(block, axis, route)  19.1 us
    all_gather x1, blocking collectives, shards(): lax.all_gather(masked_sib, 'col', axis=1, tiled=True)  10.5 us
    ppermute x3, waiting for transfers between devices, gather_around(): block = lax.ppermute(block, axis, ahead)  7.31 us
    dot_general x1, matrix products, shards(): jnp.einsum('hgp,hgd->phd', right_factor_basis, eliminated_part, preferred...  7.14 us
    ppermute x2, starting transfers between devices, swapped(): return lax.ppermute(block, axis, route)  4.88 us
  transfers between devices with their start and end apart: 8, of which 6 were waited for; matrix products, arithmetic and copies ran while one was open for 1% of the time, Pallas kernels for 0%

profile of v1, /device:TPU:0, one launch (start us, length us, event | category | flops | bytes accessed | tf_op | source)
XLA Modules:
  0.0 143.8 jit_solution(4808191163466979405)
XLA Ops:
  7.2 0.0 copy-start
  7.2 0.0 all-gather.2.cloned.1.call-start
  7.2 0.8 iota_compare_fusion
  8.0 2.1 %broadcast_select_fusion = bf16[3,512,256]{2,1,0:T(8,128)(2,1)} fusion(bf16[3,512,256]{2,1,0:T(8,128)(2,1)} %param.7, pred[3,256]{1,0:T(4,128)(4,1)S(1)} %iota_compare_fusion), kind=kLoop, calls=%fused_computation.7 | loop fusion | flops 393216 | bytes 1573632 | tf_op jit(solution)/shard_map/jit(_where)/select_n | solution.py:37
  10.1 0.0 all-gather.2.cloned.1.call-update
  10.1 0.0 copy-start.2
  10.1 0.0 reduce-scatter.2.cloned.1.call-start
  10.2 31.3 %all-gather.2.cloned.1.call-done = bf16[3,2048,256]{2,1,0:T(8,128)(2,1)} async-done(((bf16[3,512,256]{2,1,0:T(8,128)(2,1)}), bf16[3,2048,256]{2,1,0:T(8,128)(2,1)}) %all-gather.2.cloned.1.call-update) | async-done | bytes 3145744 | tf_op jit(solution)/shard_map/all_gather | solution.py:42
  41.5 7.1 %convolution_bitcast_fusion = f32[256,3,256]{2,0,1:T(8,128)} fusion(bf16[3,2048,256]{2,1,0:T(8,128)(2,1)} %all-gather.2.cloned.1.call-done, bf16[3,512,2048]{2,1,0:T(8,128)(2,1)} %param.6, bf16[3,512,256]{2,1,0:T(8,128)(2,1)} %param.8, pred[3,256]{1,0:T(4,128)(4,1)S(1)} %iota_compare_fusion), kind=kOutput, calls=%fused_computation.1 | convolution fusion | flops 1812725760 | bytes 11010816 | tf_op jit(solution)/shard_map/hgp,hgd->phd/dot_general | solution.py:47
  48.6 0.0 reduce-scatter.2.cloned.1.call-update
  48.7 0.0 all-reduce.3.cloned.1.call-start
  48.7 0.1 dynamic-slice_convert_fusion
  48.8 0.1 broadcast_in_dim.20
  48.9 0.0 copy-done.2
  48.9 0.1 constant_dynamic-update-slice_fusion.3
  49.0 0.3 collective-permute-start
  49.3 2.4 %collective-permute-start.3 = (f32[3,64,256]{2,1,0:T(8,128)S(1)}, f32[3,64,256]{2,1,0:T(8,128)S(1)}, u32[]{:S(2)}, u32[]{:S(2)}) collective-permute-start(f32[3,64,256]{2,1,0:T(8,128)S(1)} %get-tuple-element.7), channel_id=1, source_target_pairs={{0,16},{16,0},{4,20},{20,4},{8,24},{24,8},{12,28},{28,12},{1,17},{... | collective-permute-start | bytes 589832 | tf_op jit(solution)/shard_map/ppermute | solution.py:29
  51.7 2.5 %collective-permute-done = f32[3,64,256]{2,1,0:T(8,128)S(1)} collective-permute-done((f32[3,64,256]{2,1,0:T(8,128)S(1)}, f32[3,64,256]{2,1,0:T(8,128)S(1)}, u32[]{:S(2)}, u32[]{:S(2)}) %collective-permute-start) | collective-permute-done | bytes 196640 | tf_op jit(solution)/shard_map/ppermute | solution.py:18
  54.1 0.0 collective-permute-start.1
  54.1 7.3 %collective-permute-done.3 = f32[3,64,256]{2,1,0:T(8,128)S(1)} collective-permute-done((f32[3,64,256]{2,1,0:T(8,128)S(1)}, f32[3,64,256]{2,1,0:T(8,128)S(1)}, u32[]{:S(2)}, u32[]{:S(2)}) %collective-permute-start.3) | collective-permute-done | bytes 196640 | tf_op jit(solution)/shard_map/ppermute | solution.py:29
  61.4 10.5 %all_gather.7 = f32[3,256,256]{2,1,0:T(8,128)S(1)} all-gather(f32[3,64,256]{2,1,0:T(8,128)S(1)} %collective-permute-done.3), channel_id=1, replica_groups=mesh['row'=8,'col'=4] {'col'}, dimensions={1}, use_global_device_ids=true | all-gather | bytes 983040 | tf_op jit(solution)/shard_map/all_gather | solution.py:65
  71.9 0.0 copy-done
  71.9 0.6 convolution_bitcast_fusion.2
  72.6 0.0 collective-permute-done.1
  72.6 0.4 collective-permute-start.2
  73.0 0.0 copy-start.3
  73.0 4.9 %collective-permute-done.2 = f32[3,64,256]{2,1,0:T(8,128)S(1)} collective-permute-done((f32[3,64,256]{2,1,0:T(8,128)S(1)}, f32[3,64,256]{2,1,0:T(8,128)S(1)}, u32[]{:S(2)}, u32[]{:S(2)}) %collective-permute-start.2) | collective-permute-done | bytes 196640 | tf_op jit(solution)/shard_map/ppermute | solution.py:18
  77.9 0.0 reduce-scatter.2.cloned.1.call-done
  77.9 1.5 %convolution_add_fusion = f32[3,64,256]{2,1,0:T(8,128)S(1)} fusion(f32[3,64,256]{2,1,0:T(8,128)S(1)} %convolution_bitcast_fusion.2, f32[3,256,256]{2,1,0:T(8,128)S(1)} %constant_dynamic-update-slice_fusion, f32[64,3,256]{2,0,1:T(8,128)} %reduce-scatter.2.cloned.1.call-done), kind=kOutput, calls=%fused_computation.4 | convolution fusion | flops 151044096 | bytes 1376256 | tf_op jit(solution)/shard_map/nij,njk->nik/dot_general | solution.py:67
  79.5 0.0 copy-start.1
  79.5 0.8 convolution_bitcast_fusion.1
  80.3 1.3 copy.9
  81.7 0.0 all-reduce.3.cloned.1.call-update
  81.7 0.0 copy-done.3
  81.7 0.6 dynamic-slice
  82.9 37.3 %all-reduce.3.cloned.1.call-done = f32[256,3,256]{2,1,0:T(4,128)} async-done(((f32[256,3,256]{2,1,0:T(4,128)}), f32[256,3,256]{2,1,0:T(4,128)}) %all-reduce.3.cloned.1.call-update) | async-done | bytes 786448
  120.3 1.0 dynamic-slice_bitcast_fusion
  121.3 2.5 %collective-permute-start.4 = (f32[3,64,256]{2,0,1:T(4,128)S(1)}, f32[3,64,256]{2,0,1:T(4,128)S(1)}, u32[]{:S(2)}, u32[]{:S(2)}) collective-permute-start(f32[3,64,256]{2,0,1:T(4,128)S(1)} %dynamic-slice_bitcast_fusion), channel_id=1, source_target_pairs={{0,16},{16,0},{4,20},{20,4},{8,24},{24,8},{12,28},{28,12},{1,17},{... | collective-permute-start | bytes 589832 | tf_op jit(solution)/shard_map/ppermute | solution.py:29
  123.7 11.8 %collective-permute-done.4 = f32[3,64,256]{2,0,1:T(4,128)S(1)} collective-permute-done((f32[3,64,256]{2,0,1:T(4,128)S(1)}, f32[3,64,256]{2,0,1:T(4,128)S(1)}, u32[]{:S(2)}, u32[]{:S(2)}) %collective-permute-start.4) | collective-permute-done | bytes 196640 | tf_op jit(solution)/shard_map/ppermute | solution.py:29
  135.5 1.0 fusion.12
  136.6 0.7 copy.10
  137.3 0.0 copy-done.1
  (3 shorter events, 0.1 us)
Async XLA Ops:
  7.2 64.8 %copy-start = (f32[3,64,256]{2,1,0:T(8,128)S(1)}, f32[3,64,256]{2,1,0:T(8,128)}, u32[]{:S(2)}) copy-start(f32[3,64,256]{2,1,0:T(8,128)} %param.10) | copy-start | bytes 589828
  7.2 34.3 %all-gather.2.cloned.1.call-start = ((), (), s32[]{:S(2)}) async-start(), calls=%async_computation.1 | async-start | bytes 3932160 | tf_op jit(solution)/shard_map/all_gather | solution.py:42
  10.1 38.8 %copy-start.2 = (f32[3,64,256]{2,1,0:T(8,128)S(1)}, f32[3,64,256]{2,1,0:T(8,128)}, u32[]{:S(2)}) copy-start(f32[3,64,256]{2,1,0:T(8,128)} %param.9) | copy-start | bytes 589828
  10.1 67.8 %reduce-scatter.2.cloned.1.call-start = ((), (), s32[]{:S(2)}) async-start(), calls=%async_computation.2 | async-start | bytes 983040 | tf_op jit(solution)/shard_map/reduce_scatter | solution.py:46
  48.7 71.6 %all-reduce.3.cloned.1.call-start = ((), (), s32[]{:S(2)}) async-start(), calls=%async_computation.3 | async-start | bytes 2097152
  49.0 5.1 %collective-permute-start = (f32[3,64,256]{2,1,0:T(8,128)S(1)}, f32[3,64,256]{2,1,0:T(8,128)S(1)}, u32[]{:S(2)}, u32[]{:S(2)}) collective-permute-start(f32[3,64,256]{2,1,0:T(8,128)S(1)} %get-tuple-element.7), channel_id=1, source_target_pairs={{0,1},{1,2},{2,3},{3,0},{4,5},{5,6},{6,7},{7,4},{8,9},{9,10},{10,1... | collective-permute-start | bytes 589832 | tf_op jit(solution)/shard_map/ppermute | solution.py:18
  49.3 12.1 %collective-permute-start.3 = (f32[3,64,256]{2,1,0:T(8,128)S(1)}, f32[3,64,256]{2,1,0:T(8,128)S(1)}, u32[]{:S(2)}, u32[]{:S(2)}) collective-permute-start(f32[3,64,256]{2,1,0:T(8,128)S(1)} %get-tuple-element.7), channel_id=1, source_target_pairs={{0,16},{16,0},{4,20},{20,4},{8,24},{24,8},{12,28},{28,12},{1,17},{... | collective-permute-start | bytes 589832 | tf_op jit(solution)/shard_map/ppermute | solution.py:29
  54.1 18.4 %collective-permute-start.1 = (f32[3,64,256]{2,1,0:T(8,128)S(1)}, f32[3,64,256]{2,1,0:T(8,128)S(1)}, u32[]{:S(2)}, u32[]{:S(2)}) collective-permute-start(f32[3,64,256]{2,1,0:T(8,128)S(1)} %collective-permute-done), channel_id=1, source_target_pairs={{0,1},{1,2},{2,3},{3,0},{4,5},{5,6},{6,7},{7,4},{8,9},{9,10},{10,1... | collective-permute-start | bytes 589832 | tf_op jit(solution)/shard_map/ppermute | solution.py:18
  72.6 5.3 %collective-permute-start.2 = (f32[3,64,256]{2,1,0:T(8,128)S(1)}, f32[3,64,256]{2,1,0:T(8,128)S(1)}, u32[]{:S(2)}, u32[]{:S(2)}) collective-permute-start(f32[3,64,256]{2,1,0:T(8,128)S(1)} %collective-permute-done.1), channel_id=1, source_target_pairs={{0,1},{1,2},{2,3},{3,0},{4,5},{5,6},{6,7},{7,4},{8,9},{9,10},{10,1... | collective-permute-start | bytes 589832 | tf_op jit(solution)/shard_map/ppermute | solution.py:18
  73.0 8.7 %copy-start.3 = (u32[32]{0:T(128)S(1)}, u32[32]{0:T(128)}, u32[]{:S(2)}) copy-start(u32[32]{0:T(128)} %constant.55) | copy-start | bytes 388
  79.5 57.8 %copy-start.1 = (f32[3,64,256]{2,1,0:T(8,128)}, f32[3,64,256]{2,1,0:T(8,128)S(1)}, u32[]{:S(2)}) copy-start(f32[3,64,256]{2,1,0:T(8,128)S(1)} %convolution_add_fusion) | copy-start | bytes 589828
  121.3 14.3 %collective-permute-start.4 = (f32[3,64,256]{2,0,1:T(4,128)S(1)}, f32[3,64,256]{2,0,1:T(4,128)S(1)}, u32[]{:S(2)}, u32[]{:S(2)}) collective-permute-start(f32[3,64,256]{2,0,1:T(4,128)S(1)} %dynamic-slice_bitcast_fusion), channel_id=1, source_target_pairs={{0,16},{16,0},{4,20},{20,4},{8,24},{24,8},{12,28},{28,12},{1,17},{... | collective-permute-start | bytes 589832 | tf_op jit(solution)/shard_map/ppermute | solution.py:29
Sparse Core Ops, SparseCore 0:
  10.2 31.2 all-gather.1
  48.8 24.6 reduce-scatter.1
  81.8 38.4 all-reduce.2
